TPU v7x, 32 devices: a whole 2x2x4 slice. The times are simulated.
32 devices in a mesh: rows: 4 (over z), cols: 8 (over y, x, core).
Axes of the slice: x: 2, y: 2, z: 4, core: 2. Of those that a mesh axis runs over, the one named last changes fastest.
Arguments:
- right_side: float32 [256, 128, 256], P('rows', 'cols'), may hold values from -3 to 15
- initial: float32 [256, 128, 256], P('rows', 'cols'), may hold values from -0.15 to 2.15
- conduct: float32 [256, 128, 256], P('rows', 'cols'), may hold values from 0.5 to 2
Outputs:
- basis: float32 [5, 256, 128, 256], P(None, 'rows', 'cols')
- rfactor: float32 [5, 5], replicated
- updated: float32 [256, 128, 256], P('rows', 'cols')
All inputs are finite; a program needn't handle non-finite values.
Results may differ from a plain program's by a relative error of at most 0.0028.
Values sent between devices are 32-bit elements; how exact they have to be, the bound alone decides.
A program may use at most 128 MiB of HBM per device.

v0:
```python
import functools
import math

import jax
import jax.numpy as jnp
from jax import lax
from jax.experimental import pallas as pl
from jax.experimental.pallas import tpu as pltpu
from jax.sharding import PartitionSpec as P

SHIFTS = (12.0, 3.0, 21.0, 7.0)
SCALE = 8.0
LANES = 128
MESH = pl.DeviceIdType.MESH
PAIRS = [(i, j) for j in range(5) for i in range(j + 1)]
F32 = jnp.float32


def inv_sqrt(value):
    guess = lax.rsqrt(value)
    return guess * (1.5 - 0.5 * (value * guess) * guess)


def cholesky(entry, order):
    lower, inv = {}, []
    for col in range(order):
        diag = entry(col, col)
        for inner in range(col):
            diag = diag - lower[col, inner] * lower[col, inner]
        root = inv_sqrt(diag)
        inv.append(root)
        lower[col, col] = diag * root
        for row in range(col + 1, order):
            val = entry(row, col)
            for inner in range(col):
                val = val - lower[row, inner] * lower[col, inner]
            lower[row, col] = val * root
    return lower, inv


def lower_inverse(lower, inv, order):
    result = {}
    for row in range(order):
        for col in range(row):
            total = lower[row, col] * result[col, col]
            for inner in range(col + 1, row):
                total = total + lower[row, inner] * result[inner, col]
            result[row, col] = -(total * inv[row])
        result[row, row] = inv[row]
    return result


def cycle_kernel(sizes, rs_hbm, init_hbm, cond_hbm, v_out, coef_out,
                 ku, rs, v0, v1, v2, v3, v4, cx, cy, cz, cfx, cfy, fy, hx, hy,
                 g1, g2, gm, load_sem, out_sem, hs_sem, hr_sem, s1, r1, s2, r2):
    nrows, ncols, nx, ny, nz = sizes
    nh = nz // LANES
    count = nx * ny
    step_rows = 2 * ny
    vecs = (v0, v1, v2, v3, v4)
    me_r, me_c = lax.axis_index("rows"), lax.axis_index("cols")

    loads = []
    for idx, (src, dst) in enumerate(((cond_hbm, ku.at[0]), (init_hbm, ku.at[1]), (rs_hbm, rs))):
        for h in range(nh):
            loads.append(pltpu.make_async_copy(
                src.at[:, pl.ds(h * LANES, LANES)], dst.at[h, pl.ds(0, count), :],
                load_sem.at[idx, h]))
            loads[-1].start()

    barrier = pltpu.get_barrier_semaphore()
    for d in range(1, ncols):
        pl.semaphore_signal(barrier, inc=1, device_id={"cols": lax.rem(me_c + d, ncols)},
                            device_id_type=MESH)
    for d in range(1, nrows):
        pl.semaphore_signal(barrier, inc=1, device_id={"rows": lax.rem(me_r + d, nrows)},
                            device_id_type=MESH)

    zero_plane = jnp.zeros((nh, ny, LANES), F32)
    for i in range(2):
        ku[i, :, pl.ds(count, ny), :] = zero_plane
    for vec in vecs[:4]:
        vec[:, pl.ds(count, ny), :] = zero_plane
    for edge, ref, side in ((me_c == 0, hy, 0), (me_c == ncols - 1, hy, 1),
                            (me_r == 0, hx, 0), (me_r == nrows - 1, hx, 1)):
        @pl.when(edge)
        def _(ref=ref, side=side):
            for k in range(6):
                ref[k, side] = jnp.zeros(ref.shape[2:], F32)

    def strided(side):
        return pl.ds(0 if side == 0 else ny - 1, nx, stride=ny)

    def face_copies(first, num, plane):
        made = []
        ks = first if num is None else pl.ds(first, num)
        for slot, axis, me, size in ((0, "cols", me_c, ncols), (1, "cols", me_c, ncols),
                                     (2, "rows", me_r, nrows), (3, "rows", me_r, nrows)):
            side = slot % 2
            target = me + 1 if side == 0 else me - 1
            has_target = me < size - 1 if side == 0 else me > 0
            has_source = me > 0 if side == 0 else me < size - 1
            if axis == "cols":
                src, dst = fy.at[ks, 1 - side], hy.at[ks, side]
            else:
                src, dst = plane(1 - side), hx.at[ks, side]
            made.append((has_target, has_source, pltpu.make_async_remote_copy(
                src_ref=src, dst_ref=dst, send_sem=hs_sem.at[first, slot],
                recv_sem=hr_sem.at[first, slot], device_id={axis: target}, device_id_type=MESH)))
        return made

    sent = []

    def send(copies):
        sent.extend(copies)
        for has_target, _, copy in copies:
            @pl.when(has_target)
            def _(copy=copy):
                copy.start()

    def arrive(copies):
        for _, has_source, copy in copies:
            @pl.when(has_source)
            def _(copy=copy):
                copy.wait_recv()

    def plane_start(side):
        return 0 if side == 0 else count - ny

    for cp in loads[:2 * nh]:
        cp.wait()
    for i in range(2):
        for side in range(2):
            for h in range(nh):
                fy[i, side, h] = ku[i, h, strided(side), :]
    pl.semaphore_wait(barrier, ncols + nrows - 2)
    first = face_copies(0, 2, lambda side: ku.at[:, :, pl.ds(plane_start(side), ny), :])
    send(first)

    def wide(ref, base, rows):
        return jnp.concatenate([ref[h, pl.ds(base, rows), :] for h in range(nh)], axis=1)

    def put(ref, base, rows, value):
        for h in range(nh):
            ref[h, pl.ds(base, rows), :] = value[:, h * LANES:(h + 1) * LANES]

    lane = lax.broadcasted_iota(jnp.int32, (step_rows, nz), 1)
    row = lax.broadcasted_iota(jnp.int32, (step_rows, nz), 0)
    sixteenth = 0.5 / SCALE
    y_mask = jnp.where(lax.rem(row, ny) == ny - 1, 0.0, sixteenth).astype(F32)
    z_mask = jnp.where(lane == nz - 1, 0.0, sixteenth).astype(F32)
    z_edge = jnp.where((lane == nz - 1) | (lane == 0), sixteenth, 0.0).astype(F32)
    kk, uu = ku.at[0], ku.at[1]

    @pl.loop(0, count // step_rows)
    def _(i):
        base = pl.multiple_of(i * step_rows, step_rows)
        here = wide(kk, base, step_rows)
        put(cx, base, step_rows, (here + wide(kk, base + ny, step_rows)) * sixteenth)
        put(cy, base, step_rows, (here + pltpu.roll(here, step_rows - 1, 0)) * y_mask)
        put(cz, base, step_rows, (here + pltpu.roll(here, nz - 1, 1)) * z_mask)
    cx[:, pl.ds(count - ny, ny), :] = zero_plane

    def interior(src, dst, shift, residual):
        def body(i, flux_before):
            base = pl.multiple_of(i * step_rows, step_rows)
            val = wide(src, base, step_rows)
            flux_x = wide(cx, base, step_rows) * (val - wide(src, base + ny, step_rows))
            total = flux_x - jnp.concatenate([flux_before, flux_x[:step_rows - ny]], axis=0)
            flux_y = wide(cy, base, step_rows) * (val - pltpu.roll(val, step_rows - 1, 0))
            total = total + (flux_y - pltpu.roll(flux_y, 1, 0))
            flux_z = wide(cz, base, step_rows) * (val - pltpu.roll(val, nz - 1, 1))
            total = total + (flux_z - pltpu.roll(flux_z, 1, 1))
            total = total + (wide(kk, base, step_rows) * z_edge - shift) * val
            if residual:
                total = wide(rs, base, step_rows) - SCALE * total
            put(dst, base, step_rows, total)
            return flux_x[step_rows - ny:]
        lax.fori_loop(0, count // step_rows, body, jnp.zeros((ny, nz), F32))

    def corrections(k, src, dst, sign, pack):
        for side in range(2):
            at = pl.ds(plane_start(side), ny)
            dst[:, at, :] = dst[:, at, :] + sign * (cfx[side] * (src[:, at, :] - hx[k, side]))
        for side in range(2):
            for h in range(nh):
                new = dst[h, strided(side), :] + sign * (
                    cfy[side, h] * (fy[k, side, h] - hy[k, side, h]))
                dst[h, strided(side), :] = new
                if pack:
                    fy[k + 1, side, h] = new

    for cp in loads[2 * nh:]:
        cp.wait()
    interior(uu, v0, 0.0, True)
    arrive(first)
    for side in range(2):
        at = pl.ds(plane_start(side), ny)
        cfx[side] = (kk[:, at, :] + hx[0, side]) * sixteenth
        cfy[side] = (fy[0, side] + hy[0, side]) * sixteenth
    corrections(1, uu, v0, -SCALE, True)

    sums = {}

    def gram_with(k):
        def body(i, accs):
            base = pl.multiple_of(i * 16, 16)
            accs = list(accs)
            for h in range(nh):
                for sub in range(2):
                    at = pl.ds(base + 8 * sub, 8)
                    mine = vecs[k][h, at, :]
                    for j in range(k + 1):
                        other = mine if j == k else vecs[j][h, at, :]
                        accs[j] = accs[j] + mine * other
            return tuple(accs)
        accs = lax.fori_loop(0, count // 16, body,
                             tuple(jnp.zeros((8, LANES), F32) for _ in range(k + 1)), unroll=2)
        for j in range(k + 1):
            sums[j, k] = accs[j]

    outs = []

    def write_out(k):
        for h in range(nh):
            outs.append(pltpu.make_async_copy(
                vecs[k].at[h, pl.ds(0, count), :], v_out.at[k, :, pl.ds(h * LANES, LANES)],
                out_sem.at[k, h]))
            outs[-1].start()

    for k in range(4):
        vec = vecs[k]
        copies = face_copies(2 + k, None,
                             lambda side, vec=vec: vec.at[:, pl.ds(plane_start(side), ny), :])
        send(copies)
        write_out(k)
        interior(vec, vecs[k + 1], SHIFTS[k] / SCALE, False)
        gram_with(k)
        arrive(copies)
        corrections(2 + k, vec, vecs[k + 1], 1.0, k < 3)
    write_out(4)
    gram_with(4)

    def exchange(p, buf, me, size, axis, ssem, rsem, value):
        buf[p, me] = value
        for d in range(1, size):
            copy = pltpu.make_async_remote_copy(
                src_ref=buf.at[p, me], dst_ref=buf.at[p, me], send_sem=ssem.at[p, d],
                recv_sem=rsem.at[p, d], device_id={axis: lax.rem(me + d, size)},
                device_id_type=MESH)
            copy.start()
            sent.append((None, None, copy))
        for d in range(1, size):
            slot = lax.rem(me + size - d, size)
            pltpu.make_async_remote_copy(
                src_ref=buf.at[p, me], dst_ref=buf.at[p, slot], send_sem=ssem.at[p, d],
                recv_sem=rsem.at[p, d], device_id={axis: slot}, device_id_type=MESH).wait_recv()
        total = buf[p, 0]
        for i in range(1, size):
            total = total + buf[p, i]
        return total

    def all_reduce(p, values):
        for e, pair in enumerate(PAIRS):
            gm[e:e + 1, :] = jnp.sum(values[pair], axis=0, keepdims=True)
        part = exchange(p, g1, me_c, ncols, "cols", s1, r1, gm[...])
        part = exchange(p, g2, me_r, nrows, "rows", s2, r2, part)
        gm[...] = jnp.broadcast_to(jnp.sum(part, axis=1, keepdims=True), gm.shape)
        full = {pair: gm[e:e + 1, :] for e, pair in enumerate(PAIRS)}
        return lambda i, j: full[j, i]

    gm[...] = jnp.zeros(gm.shape, F32)
    low_one, inv_one = cholesky(all_reduce(0, sums), 5)
    linv_one = lower_inverse(low_one, inv_one, 5)
    splat = {key: jnp.broadcast_to(val, (8, LANES)) for key, val in linv_one.items()}

    def body(i, accs):
        base = pl.multiple_of(i * 16, 16)
        accs = list(accs)
        for h in range(nh):
            for sub in range(2):
                at = pl.ds(base + 8 * sub, 8)
                raw = [vec[h, at, :] for vec in vecs]
                ortho = []
                for r in range(5):
                    val = splat[r, 0] * raw[0]
                    for c in range(1, r + 1):
                        val = val + splat[r, c] * raw[c]
                    ortho.append(val)
                for e, (a, b) in enumerate(PAIRS):
                    accs[e] = accs[e] + ortho[a] * ortho[b]
        return tuple(accs)
    accs = lax.fori_loop(0, count // 16, body, tuple(jnp.zeros((8, LANES), F32) for _ in PAIRS))

    low_two, inv_two = cholesky(all_reduce(1, dict(zip(PAIRS, accs))), 5)
    linv_two = lower_inverse(low_two, inv_two, 5)

    def add_up(terms):
        return functools.reduce(lambda a, b: a + b, terms)

    trans = {(i, j): add_up([linv_two[i, m] * linv_one[m, j] for m in range(j, i + 1)])
             for i in range(5) for j in range(i + 1)}
    rfac = {(i, j): add_up([low_two[m, i] * low_one[j, m] for m in range(i, j + 1)])
            for i in range(5) for j in range(i, 5)}
    shifted = {}
    for k in range(4):
        for i in range(k + 2):
            val = rfac[i, k + 1] * SCALE
            shifted[i, k] = val + rfac[i, k] * SHIFTS[k] if i <= k else val
    hess = {(i, k): add_up([shifted[i, m] * trans[k, m] for m in range(max(i - 1, 0), k + 1)])
            for k in range(4) for i in range(k + 2)}
    normal = {(i, j): add_up([hess[m, i] * hess[m, j] for m in range(min(i, j) + 2)])
              for i in range(4) for j in range(i + 1)}
    low_n, inv_n = cholesky(lambda i, j: normal[i, j], 4)
    middle = []
    for i in range(4):
        val = rfac[0, 0] * hess[0, i]
        for m in range(i):
            val = val - low_n[i, m] * middle[m]
        middle.append(val * inv_n[i])
    weights = [None] * 4
    for i in range(3, -1, -1):
        val = middle[i]
        for m in range(i + 1, 4):
            val = val - low_n[m, i] * weights[m]
        weights[i] = val * inv_n[i]

    root = math.sqrt(nrows * ncols * nx * ny * nz)
    for e, (j, i) in enumerate(PAIRS):
        coef_out[e:e + 1, :] = trans[i, j] * root
    for k in range(4):
        coef_out[16 + k:17 + k, :] = weights[k] * (1.0 / root)
    one_row = lax.broadcasted_iota(jnp.int32, (1, LANES), 1)
    for i in range(5):
        line = jnp.zeros((1, LANES), F32)
        for j in range(i, 5):
            line = jnp.where(one_row == j, rfac[i, j], line)
        coef_out[24 + i:25 + i, :] = line

    for cp in outs:
        cp.wait()
    for has_target, _, copy in sent:
        if has_target is None:
            copy.wait_send()
        else:
            @pl.when(has_target)
            def _(copy=copy):
                copy.wait_send()


def finish_kernel(v_ref, init_ref, coef_ref, basis_ref, rfac_ref, updated_ref):
    rows, nz = init_ref.shape
    trans = {(i, j): jnp.broadcast_to(coef_ref[e:e + 1, :], (8, LANES))
             for e, (j, i) in enumerate(PAIRS)}
    weights = [jnp.broadcast_to(coef_ref[16 + k:17 + k, :], (8, LANES)) for k in range(4)]

    def body(n, carry):
        at = pl.ds(pl.multiple_of(n * 8, 8), 8)
        for h in range(nz // LANES):
            lanes = pl.ds(h * LANES, LANES)
            raw = [v_ref[k, at, lanes] for k in range(5)]
            new = init_ref[at, lanes]
            for i in range(5):
                val = trans[i, 0] * raw[0]
                for j in range(1, i + 1):
                    val = val + trans[i, j] * raw[j]
                basis_ref[i, at, lanes] = val
                if i < 4:
                    new = new + weights[i] * val
            updated_ref[at, lanes] = new
        return carry
    lax.fori_loop(0, rows // 8, body, 0, unroll=2)
    rfac_ref[...] = coef_ref[24:29, 0:5]


def on_device(nrows, ncols, right_side, initial, conduct):
    nx, ny, nz = initial.shape
    nh, count = nz // LANES, nx * ny
    flat = [a.reshape(count, nz) for a in (right_side, initial, conduct)]
    dma = pltpu.SemaphoreType.DMA
    vec = pltpu.VMEM((nh, count + ny, LANES), F32)
    plain = pltpu.VMEM((nh, count, LANES), F32)
    vectors, coefs = pl.pallas_call(
        functools.partial(cycle_kernel, (nrows, ncols, nx, ny, nz)),
        out_shape=(jax.ShapeDtypeStruct((5, count, nz), F32),
                   jax.ShapeDtypeStruct((32, LANES), F32)),
        in_specs=[pl.BlockSpec(memory_space=pl.ANY)] * 3,
        out_specs=(pl.BlockSpec(memory_space=pl.ANY), pl.BlockSpec(memory_space=pltpu.VMEM)),
        scratch_shapes=[
            pltpu.VMEM((2, nh, count + ny, LANES), F32), plain, vec, vec, vec, vec, plain,
            plain, plain, plain,
            pltpu.VMEM((2, nh, ny, LANES), F32), pltpu.VMEM((2, nh, nx, LANES), F32),
            pltpu.VMEM((6, 2, nh, nx, LANES), F32),
            pltpu.VMEM((6, 2, nh, ny, LANES), F32), pltpu.VMEM((6, 2, nh, nx, LANES), F32),
            pltpu.VMEM((2, ncols, 16, LANES), F32), pltpu.VMEM((2, nrows, 16, LANES), F32),
            pltpu.VMEM((16, LANES), F32),
            dma((3, nh)), dma((5, nh)), dma((6, 4)), dma((6, 4)),
            dma((2, ncols)), dma((2, ncols)), dma((2, nrows)), dma((2, nrows)),
        ],
        compiler_params=pltpu.CompilerParams(
            collective_id=0, has_side_effects=True, vmem_limit_bytes=40 << 20),
        name="cycle",
    )(*flat)
    block = 128
    basis, rfactor, updated = pl.pallas_call(
        finish_kernel,
        grid=(count // block,),
        out_shape=(jax.ShapeDtypeStruct((5, count, nz), F32),
                   jax.ShapeDtypeStruct((5, 5), F32),
                   jax.ShapeDtypeStruct((count, nz), F32)),
        in_specs=[pl.BlockSpec((5, block, nz), lambda i: (0, i, 0)),
                  pl.BlockSpec((block, nz), lambda i: (i, 0)),
                  pl.BlockSpec((32, LANES), lambda i: (0, 0))],
        out_specs=(pl.BlockSpec((5, block, nz), lambda i: (0, i, 0)),
                   pl.BlockSpec((5, 5), lambda i: (0, 0)),
                   pl.BlockSpec((block, nz), lambda i: (i, 0))),
        compiler_params=pltpu.CompilerParams(vmem_limit_bytes=40 << 20),
        name="finish",
    )(vectors, flat[1], coefs)
    return (basis.reshape(5, nx, ny, nz), rfactor, updated.reshape(nx, ny, nz))


def solution(mesh):
    nrows, ncols = mesh.shape["rows"], mesh.shape["cols"]
    return jax.shard_map(
        functools.partial(on_device, nrows, ncols),
        mesh=mesh,
        in_specs=(P("rows", "cols", None),) * 3,
        out_specs=(P(None, "rows", "cols", None), P(), P("rows", "cols", None)),
        check_vma=False,
    )
```

profile of v0, /device:TPU:0, one launch (start us, length us, event | category | flops | bytes accessed | tf_op | source)
XLA Modules:
  0.0 62.4 jit_solution(3160730547832887479)
XLA Ops:
  0.6 0.0 copy-start
  0.6 1.2 %copy-done = f32[64,16,256]{2,1,0:T(8,128)S(1)} copy-done((f32[64,16,256]{2,1,0:T(8,128)S(1)}, f32[64,16,256]{2,1,0:T(8,128)}, u32[]{:S(2)}) %copy-start) | copy-done | bytes 1048600
  1.9 0.0 copy-start.1
  1.9 1.2 %copy-done.1 = f32[64,16,256]{2,1,0:T(8,128)S(1)} copy-done((f32[64,16,256]{2,1,0:T(8,128)S(1)}, f32[64,16,256]{2,1,0:T(8,128)}, u32[]{:S(2)}) %copy-start.1) | copy-done | bytes 1048600
  3.1 0.0 copy-start.2
  3.1 1.2 %copy-done.2 = f32[64,16,256]{2,1,0:T(8,128)S(1)} copy-done((f32[64,16,256]{2,1,0:T(8,128)S(1)}, f32[64,16,256]{2,1,0:T(8,128)}, u32[]{:S(2)}) %copy-start.2) | copy-done | bytes 1048600
  4.3 53.3 %cycle.1 = (f32[5,1024,256]{2,1,0:T(8,128)S(1)}, f32[32,128]{1,0:T(8,128)S(1)}) custom-call(f32[1024,256]{1,0:T(8,128)S(1)} %bitcast.7, f32[1024,256]{1,0:T(8,128)S(1)} %bitcast.5, f32[1024,256]{1,0:T(8,128)S(1)} %bitcast.8), custom_call_target="tpu_custom_call" | custom-call | tf_op jit(solution)/shard_map/cycle/pallas_call | solution.py:383
  57.6 4.8 %finish.1 = (f32[5,1024,256]{2,1,0:T(8,128)}, f32[5,5]{1,0:T(8,128)}, f32[1024,256]{1,0:T(8,128)}) custom-call(f32[5,1024,256]{2,1,0:T(8,128)S(1)} %get-tuple-element.8.v_ref, f32[1024,256]{1,0:T(8,128)S(1)} %bitcast.6, f32[32,128]{1,0:T(8,128)S(1)} %get-tuple-element.9.coef_ref), custom_call_target="tpu_custom_call" | custom-call | tf_op jit(solution)/shard_map/finish/pallas_call | solution.py:405
Async XLA Ops:
  0.6 1.2 %copy-start = (f32[64,16,256]{2,1,0:T(8,128)S(1)}, f32[64,16,256]{2,1,0:T(8,128)}, u32[]{:S(2)}) copy-start(f32[64,16,256]{2,1,0:T(8,128)} %param.4) | copy-start | bytes 3145732
  1.9 1.2 %copy-start.1 = (f32[64,16,256]{2,1,0:T(8,128)S(1)}, f32[64,16,256]{2,1,0:T(8,128)}, u32[]{:S(2)}) copy-start(f32[64,16,256]{2,1,0:T(8,128)} %param.3) | copy-start | bytes 3145732
  3.1 1.2 %copy-start.2 = (f32[64,16,256]{2,1,0:T(8,128)S(1)}, f32[64,16,256]{2,1,0:T(8,128)}, u32[]{:S(2)}) copy-start(f32[64,16,256]{2,1,0:T(8,128)} %param.5) | copy-start | bytes 3145732
where the time goes:
time: 62.6 us; the launch traced here: 62.4 us
  Pallas kernels  58.1 us (93%)
  local copies, waits for them, and re-layouts  3.67 us (6%)
  between operations  0.65 us (1%)
    pallas_call x1, Pallas kernels, on_device(): pl.pallas_call(functools.partial(cycle_kernel, (nrows, ncols, nx, ny, nz)...  53.3 us
    pallas_call x1, Pallas kernels, on_device(): pl.pallas_call(finish_kernel, grid=(count // block,), out_shape=(jax.Shap...  4.77 us
    unnamed x6, local copies, waits for them, and re-layouts  3.67 us

commit v1 on v0

--- a/solution.py
+++ b/solution.py
@@ -51,12 +51,13 @@
 
 
 def cycle_kernel(sizes, rs_hbm, init_hbm, cond_hbm, v_out, coef_out,
-                 ku, rs, v0, v1, v2, v3, v4, cx, cy, cz, cfx, cfy, fy, hx, hy,
+                 ku, rs, v0, v1, v2, v3, v4, cx, cy, cyb, cz, czb, cfx, cfy, fy, hx, hy,
                  g1, g2, gm, load_sem, out_sem, hs_sem, hr_sem, s1, r1, s2, r2):
     nrows, ncols, nx, ny, nz = sizes
     nh = nz // LANES
     count = nx * ny
-    step_rows = 2 * ny
+    step_rows = 4 * ny
+    one_stage = nrows * ncols <= 64
     vecs = (v0, v1, v2, v3, v4)
     me_r, me_c = lax.axis_index("rows"), lax.axis_index("cols")
 
@@ -69,12 +70,12 @@
             loads[-1].start()
 
     barrier = pltpu.get_barrier_semaphore()
-    for d in range(1, ncols):
-        pl.semaphore_signal(barrier, inc=1, device_id={"cols": lax.rem(me_c + d, ncols)},
-                            device_id_type=MESH)
-    for d in range(1, nrows):
-        pl.semaphore_signal(barrier, inc=1, device_id={"rows": lax.rem(me_r + d, nrows)},
-                            device_id_type=MESH)
+    everyone = [(dr, dc) for dr in range(nrows) for dc in range(ncols)][1:]
+    greeted = everyone if one_stage else (
+        [(0, d) for d in range(1, ncols)] + [(d, 0) for d in range(1, nrows)])
+    for dr, dc in greeted:
+        pl.semaphore_signal(barrier, inc=1, device_id_type=MESH,
+                            device_id=(lax.rem(me_r + dr, nrows), lax.rem(me_c + dc, ncols)))
 
     zero_plane = jnp.zeros((nh, ny, LANES), F32)
     for i in range(2):
@@ -133,7 +134,7 @@
         for side in range(2):
             for h in range(nh):
                 fy[i, side, h] = ku[i, h, strided(side), :]
-    pl.semaphore_wait(barrier, ncols + nrows - 2)
+    pl.semaphore_wait(barrier, len(greeted))
     first = face_copies(0, 2, lambda side: ku.at[:, :, pl.ds(plane_start(side), ny), :])
     send(first)
 
@@ -157,8 +158,12 @@
         base = pl.multiple_of(i * step_rows, step_rows)
         here = wide(kk, base, step_rows)
         put(cx, base, step_rows, (here + wide(kk, base + ny, step_rows)) * sixteenth)
-        put(cy, base, step_rows, (here + pltpu.roll(here, step_rows - 1, 0)) * y_mask)
-        put(cz, base, step_rows, (here + pltpu.roll(here, nz - 1, 1)) * z_mask)
+        above = (here + pltpu.roll(here, step_rows - 1, 0)) * y_mask
+        put(cy, base, step_rows, above)
+        put(cyb, base, step_rows, pltpu.roll(above, 1, 0))
+        after = (here + pltpu.roll(here, nz - 1, 1)) * z_mask
+        put(cz, base, step_rows, after)
+        put(czb, base, step_rows, pltpu.roll(after, 1, 1))
     cx[:, pl.ds(count - ny, ny), :] = zero_plane
 
     def interior(src, dst, shift, residual):
@@ -167,10 +172,10 @@
             val = wide(src, base, step_rows)
             flux_x = wide(cx, base, step_rows) * (val - wide(src, base + ny, step_rows))
             total = flux_x - jnp.concatenate([flux_before, flux_x[:step_rows - ny]], axis=0)
-            flux_y = wide(cy, base, step_rows) * (val - pltpu.roll(val, step_rows - 1, 0))
-            total = total + (flux_y - pltpu.roll(flux_y, 1, 0))
-            flux_z = wide(cz, base, step_rows) * (val - pltpu.roll(val, nz - 1, 1))
-            total = total + (flux_z - pltpu.roll(flux_z, 1, 1))
+            total = total + wide(cy, base, step_rows) * (val - pltpu.roll(val, step_rows - 1, 0))
+            total = total + wide(cyb, base, step_rows) * (val - pltpu.roll(val, 1, 0))
+            total = total + wide(cz, base, step_rows) * (val - pltpu.roll(val, nz - 1, 1))
+            total = total + wide(czb, base, step_rows) * (val - pltpu.roll(val, 1, 1))
             total = total + (wide(kk, base, step_rows) * z_edge - shift) * val
             if residual:
                 total = wide(rs, base, step_rows) - SCALE * total
@@ -241,31 +246,52 @@
     write_out(4)
     gram_with(4)
 
-    def exchange(p, buf, me, size, axis, ssem, rsem, value):
-        buf[p, me] = value
-        for d in range(1, size):
+    def exchange(p, buf, ssem, rsem, peers, slot, value):
+        buf[p, slot(0, 0)] = value
+        for e, (dr, dc) in enumerate(peers):
             copy = pltpu.make_async_remote_copy(
-                src_ref=buf.at[p, me], dst_ref=buf.at[p, me], send_sem=ssem.at[p, d],
-                recv_sem=rsem.at[p, d], device_id={axis: lax.rem(me + d, size)},
+                src_ref=buf.at[p, slot(0, 0)], dst_ref=buf.at[p, slot(0, 0)],
+                send_sem=ssem.at[p, e], recv_sem=rsem.at[p, e],
+                device_id=(lax.rem(me_r + dr, nrows), lax.rem(me_c + dc, ncols)),
                 device_id_type=MESH)
             copy.start()
             sent.append((None, None, copy))
-        for d in range(1, size):
-            slot = lax.rem(me + size - d, size)
+        for e, (dr, dc) in enumerate(peers):
             pltpu.make_async_remote_copy(
-                src_ref=buf.at[p, me], dst_ref=buf.at[p, slot], send_sem=ssem.at[p, d],
-                recv_sem=rsem.at[p, d], device_id={axis: slot}, device_id_type=MESH).wait_recv()
-        total = buf[p, 0]
-        for i in range(1, size):
-            total = total + buf[p, i]
-        return total
+                src_ref=buf.at[p, slot(0, 0)], dst_ref=buf.at[p, slot(nrows - dr, ncols - dc)],
+                send_sem=ssem.at[p, e], recv_sem=rsem.at[p, e],
+                device_id=(lax.rem(me_r + nrows - dr, nrows), lax.rem(me_c + ncols - dc, ncols)),
+                device_id_type=MESH).wait_recv()
+        parts = [buf[p, i] for i in range(len(peers) + 1)]
+        while len(parts) > 1:
+            parts = [a + b for a, b in zip(parts[::2], parts[1::2])] + (
+                parts[-1:] if len(parts) % 2 else [])
+        return parts[0]
+
+    def col_of(dc):
+        return lax.rem(me_c + dc, ncols)
+
+    def row_of(dr):
+        return lax.rem(me_r + dr, nrows)
+
+    pair_row = lax.broadcasted_iota(jnp.int32, (16, LANES), 0)
+    on_diag = pair_row == lax.broadcasted_iota(jnp.int32, (16, LANES), 1)
 
     def all_reduce(p, values):
         for e, pair in enumerate(PAIRS):
             gm[e:e + 1, :] = jnp.sum(values[pair], axis=0, keepdims=True)
-        part = exchange(p, g1, me_c, ncols, "cols", s1, r1, gm[...])
-        part = exchange(p, g2, me_r, nrows, "rows", s2, r2, part)
-        gm[...] = jnp.broadcast_to(jnp.sum(part, axis=1, keepdims=True), gm.shape)
+        line = jnp.sum(jnp.where(on_diag, jnp.sum(gm[...], axis=1, keepdims=True), 0.0),
+                       axis=0, keepdims=True)
+        if one_stage:
+            line = exchange(p, g1, s1, r1, everyone,
+                            lambda dr, dc: row_of(dr) * ncols + col_of(dc), line)
+        else:
+            line = exchange(p, g1, s1, r1, [(0, d) for d in range(1, ncols)],
+                            lambda dr, dc: col_of(dc), line)
+            line = exchange(p, g2, s2, r2, [(d, 0) for d in range(1, nrows)],
+                            lambda dr, dc: row_of(dr), line)
+        gm[...] = jnp.broadcast_to(
+            jnp.sum(jnp.where(on_diag, line, 0.0), axis=1, keepdims=True), gm.shape)
         full = {pair: gm[e:e + 1, :] for e, pair in enumerate(PAIRS)}
         return lambda i, j: full[j, i]
 
@@ -290,7 +316,7 @@
                 for e, (a, b) in enumerate(PAIRS):
                     accs[e] = accs[e] + ortho[a] * ortho[b]
         return tuple(accs)
-    accs = lax.fori_loop(0, count // 16, body, tuple(jnp.zeros((8, LANES), F32) for _ in PAIRS))
+    accs = lax.fori_loop(0, count // 16, body, tuple(jnp.zeros((8, LANES), F32) for _ in PAIRS), unroll=2)
 
     low_two, inv_two = cholesky(all_reduce(1, dict(zip(PAIRS, accs))), 5)
     linv_two = lower_inverse(low_two, inv_two, 5)
@@ -309,20 +335,23 @@
             shifted[i, k] = val + rfac[i, k] * SHIFTS[k] if i <= k else val
     hess = {(i, k): add_up([shifted[i, m] * trans[k, m] for m in range(max(i - 1, 0), k + 1)])
             for k in range(4) for i in range(k + 2)}
-    normal = {(i, j): add_up([hess[m, i] * hess[m, j] for m in range(min(i, j) + 2)])
-              for i in range(4) for j in range(i + 1)}
-    low_n, inv_n = cholesky(lambda i, j: normal[i, j], 4)
-    middle = []
-    for i in range(4):
-        val = rfac[0, 0] * hess[0, i]
-        for m in range(i):
-            val = val - low_n[i, m] * middle[m]
-        middle.append(val * inv_n[i])
+    target, inv_n = [rfac[0, 0]], []
+    for k in range(4):
+        top, bottom = hess[k, k], hess[k + 1, k]
+        square = top * top + bottom * bottom
+        inv_n.append(inv_sqrt(square))
+        cosine, sine = top * inv_n[k], bottom * inv_n[k]
+        for j in range(k + 1, 4):
+            upper, under = hess[k, j], hess[k + 1, j]
+            hess[k, j] = cosine * upper + sine * under
+            hess[k + 1, j] = cosine * under - sine * upper
+        target.append(-(sine * target[k]))
+        target[k] = cosine * target[k]
     weights = [None] * 4
     for i in range(3, -1, -1):
-        val = middle[i]
+        val = target[i]
         for m in range(i + 1, 4):
-            val = val - low_n[m, i] * weights[m]
+            val = val - hess[i, m] * weights[m]
         weights[i] = val * inv_n[i]
 
     root = math.sqrt(nrows * ncols * nx * ny * nz)
@@ -369,7 +398,7 @@
                     new = new + weights[i] * val
             updated_ref[at, lanes] = new
         return carry
-    lax.fori_loop(0, rows // 8, body, 0, unroll=2)
+    lax.fori_loop(0, rows // 8, body, 0, unroll=4)
     rfac_ref[...] = coef_ref[24:29, 0:5]
 
 
@@ -378,30 +407,31 @@
     nh, count = nz // LANES, nx * ny
     flat = [a.reshape(count, nz) for a in (right_side, initial, conduct)]
     dma = pltpu.SemaphoreType.DMA
+    slots = nrows * ncols
     vec = pltpu.VMEM((nh, count + ny, LANES), F32)
     plain = pltpu.VMEM((nh, count, LANES), F32)
     vectors, coefs = pl.pallas_call(
         functools.partial(cycle_kernel, (nrows, ncols, nx, ny, nz)),
         out_shape=(jax.ShapeDtypeStruct((5, count, nz), F32),
                    jax.ShapeDtypeStruct((32, LANES), F32)),
-        in_specs=[pl.BlockSpec(memory_space=pl.ANY)] * 3,
+        in_specs=[pl.BlockSpec(memory_space=pltpu.HBM)] * 3,
         out_specs=(pl.BlockSpec(memory_space=pl.ANY), pl.BlockSpec(memory_space=pltpu.VMEM)),
         scratch_shapes=[
             pltpu.VMEM((2, nh, count + ny, LANES), F32), plain, vec, vec, vec, vec, plain,
-            plain, plain, plain,
+            plain, plain, plain, plain, plain,
             pltpu.VMEM((2, nh, ny, LANES), F32), pltpu.VMEM((2, nh, nx, LANES), F32),
             pltpu.VMEM((6, 2, nh, nx, LANES), F32),
             pltpu.VMEM((6, 2, nh, ny, LANES), F32), pltpu.VMEM((6, 2, nh, nx, LANES), F32),
-            pltpu.VMEM((2, ncols, 16, LANES), F32), pltpu.VMEM((2, nrows, 16, LANES), F32),
+            pltpu.VMEM((2, slots, 1, LANES), F32), pltpu.VMEM((2, nrows, 1, LANES), F32),
             pltpu.VMEM((16, LANES), F32),
             dma((3, nh)), dma((5, nh)), dma((6, 4)), dma((6, 4)),
-            dma((2, ncols)), dma((2, ncols)), dma((2, nrows)), dma((2, nrows)),
+            dma((2, slots)), dma((2, slots)), dma((2, nrows)), dma((2, nrows)),
         ],
         compiler_params=pltpu.CompilerParams(
-            collective_id=0, has_side_effects=True, vmem_limit_bytes=40 << 20),
+            collective_id=0, has_side_effects=True, vmem_limit_bytes=60 << 20),
         name="cycle",
     )(*flat)
-    block = 128
+    block = 256
     basis, rfactor, updated = pl.pallas_call(
         finish_kernel,
         grid=(count // block,),
@@ -414,7 +444,7 @@
         out_specs=(pl.BlockSpec((5, block, nz), lambda i: (0, i, 0)),
                    pl.BlockSpec((5, 5), lambda i: (0, 0)),
                    pl.BlockSpec((block, nz), lambda i: (i, 0))),
-        compiler_params=pltpu.CompilerParams(vmem_limit_bytes=40 << 20),
+        compiler_params=pltpu.CompilerParams(vmem_limit_bytes=60 << 20),
         name="finish",
     )(vectors, flat[1], coefs)
     return (basis.reshape(5, nx, ny, nz), rfactor, updated.reshape(nx, ny, nz))

time: 62.6 us -> 47.1 us (0.75)
  Pallas kernels: 58.1 us -> 46.2 us
  local copies, waits for them, and re-layouts: 3.67 us -> 0 us
    pallas_call x1, Pallas kernels: 53.3 us -> 39.9 us  [on_device(): pl.pallas_call(functools.partial(cycle_kernel, (nrows, ncols, nx, ny, nz)...]
    unnamed x6 -> x0, local copies, waits for them, and re-layouts: 3.67 us -> none
    pallas_call x1, Pallas kernels: 4.77 us -> 6.32 us  [on_device(): pl.pallas_call(finish_kernel, grid=(count // block,), out_shape=(jax.Shap...]
where the time goes in v1:
time: 47.1 us; the launch traced here: 46.9 us
  Pallas kernels  46.2 us (98%)
  between operations  0.64 us (1%)
    pallas_call x1, Pallas kernels, on_device(): pl.pallas_call(functools.partial(cycle_kernel, (nrows, ncols, nx, ny, nz)...  39.9 us
    pallas_call x1, Pallas kernels, on_device(): pl.pallas_call(finish_kernel, grid=(count // block,), out_shape=(jax.Shap...  6.32 us

profile of v1, /device:TPU:0, one launch (start us, length us, event | category | flops | bytes accessed | tf_op | source)
XLA Modules:
  0.0 46.9 jit_solution(178617627067397467)
XLA Ops:
  0.6 39.9 %cycle.1 = (f32[5,1024,256]{2,1,0:T(8,128)}, f32[32,128]{1,0:T(8,128)}) custom-call(f32[1024,256]{1,0:T(8,128)} %bitcast.7, f32[1024,256]{1,0:T(8,128)} %bitcast.5, f32[1024,256]{1,0:T(8,128)} %bitcast.8), custom_call_target="tpu_custom_call" | custom-call | tf_op jit(solution)/shard_map/cycle/pallas_call | solution.py:413
  40.6 6.3 %finish.1 = (f32[5,1024,256]{2,1,0:T(8,128)}, f32[5,5]{1,0:T(8,128)}, f32[1024,256]{1,0:T(8,128)}) custom-call(f32[5,1024,256]{2,1,0:T(8,128)} %get-tuple-element.8.v_ref, f32[1024,256]{1,0:T(8,128)} %bitcast.6, f32[32,128]{1,0:T(8,128)} %get-tuple-element.9.coef_ref), custom_call_target="tpu_custom_call" | custom-call | tf_op jit(solution)/shard_map/finish/pallas_call | solution.py:435

commit v2 on v1

--- a/solution.py
+++ b/solution.py
@@ -229,10 +229,11 @@
     def write_out(k):
         for h in range(nh):
             outs.append(pltpu.make_async_copy(
-                vecs[k].at[h, pl.ds(0, count), :], v_out.at[k, :, pl.ds(h * LANES, LANES)],
+                (vecs[k] if k < 5 else uu).at[h, pl.ds(0, count), :], v_out.at[k, :, pl.ds(h * LANES, LANES)],
                 out_sem.at[k, h]))
             outs[-1].start()
 
+    write_out(5)
     for k in range(4):
         vec = vecs[k]
         copies = face_copies(2 + k, None,
@@ -377,8 +378,8 @@
                 copy.wait_send()
 
 
-def finish_kernel(v_ref, init_ref, coef_ref, basis_ref, rfac_ref, updated_ref):
-    rows, nz = init_ref.shape
+def finish_kernel(v_ref, coef_ref, basis_ref, rfac_ref, updated_ref):
+    _, rows, nz = v_ref.shape
     trans = {(i, j): jnp.broadcast_to(coef_ref[e:e + 1, :], (8, LANES))
              for e, (j, i) in enumerate(PAIRS)}
     weights = [jnp.broadcast_to(coef_ref[16 + k:17 + k, :], (8, LANES)) for k in range(4)]
@@ -388,7 +389,7 @@
         for h in range(nz // LANES):
             lanes = pl.ds(h * LANES, LANES)
             raw = [v_ref[k, at, lanes] for k in range(5)]
-            new = init_ref[at, lanes]
+            new = v_ref[5, at, lanes]
             for i in range(5):
                 val = trans[i, 0] * raw[0]
                 for j in range(1, i + 1):
@@ -412,8 +413,8 @@
     plain = pltpu.VMEM((nh, count, LANES), F32)
     vectors, coefs = pl.pallas_call(
         functools.partial(cycle_kernel, (nrows, ncols, nx, ny, nz)),
-        out_shape=(jax.ShapeDtypeStruct((5, count, nz), F32),
-                   jax.ShapeDtypeStruct((32, LANES), F32)),
+        out_shape=(pltpu.VMEM((6, count, nz), F32),
+                   pltpu.VMEM((32, LANES), F32)),
         in_specs=[pl.BlockSpec(memory_space=pltpu.HBM)] * 3,
         out_specs=(pl.BlockSpec(memory_space=pl.ANY), pl.BlockSpec(memory_space=pltpu.VMEM)),
         scratch_shapes=[
@@ -424,11 +425,11 @@
             pltpu.VMEM((6, 2, nh, ny, LANES), F32), pltpu.VMEM((6, 2, nh, nx, LANES), F32),
             pltpu.VMEM((2, slots, 1, LANES), F32), pltpu.VMEM((2, nrows, 1, LANES), F32),
             pltpu.VMEM((16, LANES), F32),
-            dma((3, nh)), dma((5, nh)), dma((6, 4)), dma((6, 4)),
+            dma((3, nh)), dma((6, nh)), dma((6, 4)), dma((6, 4)),
             dma((2, slots)), dma((2, slots)), dma((2, nrows)), dma((2, nrows)),
         ],
         compiler_params=pltpu.CompilerParams(
-            collective_id=0, has_side_effects=True, vmem_limit_bytes=60 << 20),
+            collective_id=0, has_side_effects=True, vmem_limit_bytes=56 << 20),
         name="cycle",
     )(*flat)
     block = 256
@@ -438,15 +439,14 @@
         out_shape=(jax.ShapeDtypeStruct((5, count, nz), F32),
                    jax.ShapeDtypeStruct((5, 5), F32),
                    jax.ShapeDtypeStruct((count, nz), F32)),
-        in_specs=[pl.BlockSpec((5, block, nz), lambda i: (0, i, 0)),
-                  pl.BlockSpec((block, nz), lambda i: (i, 0)),
+        in_specs=[pl.BlockSpec((6, block, nz), lambda i: (0, i, 0)),
                   pl.BlockSpec((32, LANES), lambda i: (0, 0))],
         out_specs=(pl.BlockSpec((5, block, nz), lambda i: (0, i, 0)),
                    pl.BlockSpec((5, 5), lambda i: (0, 0)),
                    pl.BlockSpec((block, nz), lambda i: (i, 0))),
-        compiler_params=pltpu.CompilerParams(vmem_limit_bytes=60 << 20),
+        compiler_params=pltpu.CompilerParams(vmem_limit_bytes=20 << 20),
         name="finish",
-    )(vectors, flat[1], coefs)
+    )(vectors, coefs)
     return (basis.reshape(5, nx, ny, nz), rfactor, updated.reshape(nx, ny, nz))
 
 

time: 47.1 us -> 44.1 us (0.936)
  Pallas kernels: 46.2 us -> 43.3 us
    pallas_call x1, Pallas kernels: 6.32 us -> 3.81 us  [on_device(): pl.pallas_call(finish_kernel, grid=(count // block,), out_shape=(jax.Shap...]
where the time goes in v2:
time: 44.1 us; the launch traced here: 43.9 us
  Pallas kernels  43.3 us (98%)
  between operations  0.64 us (1%)
    pallas_call x1, Pallas kernels, on_device(): pl.pallas_call(functools.partial(cycle_kernel, (nrows, ncols, nx, ny, nz)...  39.5 us
    pallas_call x1, Pallas kernels, on_device(): pl.pallas_call(finish_kernel, grid=(count // block,), out_shape=(jax.Shap...  3.81 us

profile of v2, /device:TPU:0, one launch (start us, length us, event | category | flops | bytes accessed | tf_op | source)
XLA Modules:
  0.0 43.9 jit_solution(7685857369096961064)
XLA Ops:
  0.6 39.5 %cycle.1 = (f32[6,1024,256]{2,1,0:T(8,128)S(1)}, f32[32,128]{1,0:T(8,128)S(1)}) custom-call(f32[1024,256]{1,0:T(8,128)} %bitcast.5, f32[1024,256]{1,0:T(8,128)} %bitcast.6, f32[1024,256]{1,0:T(8,128)} %bitcast.7), custom_call_target="tpu_custom_call" | custom-call | tf_op jit(solution)/shard_map/cycle/pallas_call | solution.py:414
  40.1 3.8 %finish.1 = (f32[5,1024,256]{2,1,0:T(8,128)}, f32[5,5]{1,0:T(8,128)}, f32[1024,256]{1,0:T(8,128)}) custom-call(f32[6,1024,256]{2,1,0:T(8,128)S(1)} %get-tuple-element.8.v_ref, f32[32,128]{1,0:T(8,128)S(1)} %get-tuple-element.9.coef_ref), custom_call_target="tpu_custom_call" | custom-call | tf_op jit(solution)/shard_map/finish/pallas_call | solution.py:436
